TPU v7x, 512 devices: a whole 4x8x8 slice. The times are simulated.
512 devices in a mesh: seq: 64 (over z, x, core), mp: 8 (over y).
Axes of the slice: x: 4, y: 8, z: 8, core: 2. Of those that a mesh axis runs over, the one named last changes fastest.
Arguments:
- tokens: bfloat16 [32768, 1792], P('seq'), may hold values from -400 to 400, as said below
- norm_gain: float32 [1792], replicated, may hold values from 0.1 to 1.9
- q_weight: bfloat16 [1792, 256], P(None, 'mp'), may hold values from -0.125 to 0.125
- k_weight: bfloat16 [1792, 256], P(None, 'mp'), may hold values from -0.125 to 0.125
- v_weight: bfloat16 [1792, 1792], P(None, 'mp'), may hold values from -0.125 to 0.125
- out_gain: float32 [1792], P('mp'), may hold values from 0.1 to 1.9
- o_weight: bfloat16 [1792, 1792], P('mp'), may hold values from -0.125 to 0.125
- lengths: int32 [8], replicated, may hold values from 1 to 16384, 32768 in all
Outputs:
- mixed: bfloat16 [32768, 1792], P('seq', 'mp')
Inputs may be any that keep to these rules, and one draw needn't show every extreme that they name: The lengths sum to 32768; the longest is exactly 16384. `tokens`: finite hidden states.
All inputs are finite; a program needn't handle non-finite values.
Results may differ from a plain program's by a relative error of at most 0.02.
Values may be sent and summed in bfloat16 or wider, within the bound.
A program may use at most 64 MiB of HBM per device.

v0:
```python
import math

import jax
import jax.numpy as jnp
from jax import lax
from jax.sharding import PartitionSpec as P

FEAT = 16


def entering(shard, axis, combine, identity):
    count, index = (lax.axis_size(axis), lax.axis_index(axis))
    everything = jax.tree.map(
        lambda part, kind: lax.all_gather(part.astype(kind), axis),
        shard,
        (jnp.bfloat16, jnp.bfloat16, jnp.bfloat16),
    )
    start = jax.tree.map(
        lambda part, zero: jnp.broadcast_to(jnp.asarray(zero, part.dtype), part.shape),
        shard,
        identity,
    )

    def lap(k, before):
        reached = k < index
        new = combine(
            before, jax.tree.map(lambda part, own: part[k].astype(own.dtype), everything, shard)
        )
        return jax.tree.map(lambda a, b: jnp.where(reached, a, b), new, before)

    return lax.fori_loop(0, count, lap, start)


def doc_starts(positions, lengths):
    doc_ends = jnp.cumsum(lengths)
    finished = doc_ends[None, :] <= positions[:, None]
    return jnp.sum(jnp.where(finished, lengths[None, :], 0), axis=1)


def rms_norm(rows_in, gain_vec):
    widened = rows_in.astype(jnp.float32)
    row_scale = lax.rsqrt(jnp.mean(widened * widened, axis=-1, keepdims=True) + 1e-06)
    return widened * row_scale * gain_vec


def features(projected, head_count):
    row_count = projected.shape[0]
    feat_width = projected.shape[1] // head_count
    split_proj = projected.reshape(row_count, head_count, feat_width)
    linear_part = split_proj * feat_width ** (-0.25)
    square_part = (split_proj[..., :, None] * split_proj[..., None, :]).reshape(
        row_count, head_count, feat_width * feat_width
    )
    square_part = square_part * (1.0 / (math.sqrt(2.0) * math.sqrt(feat_width)))
    constant = jnp.ones((row_count, head_count, 1), split_proj.dtype)
    return jnp.concatenate([constant, linear_part, square_part], axis=-1).astype(jnp.bfloat16)


def head_gain(attended, gain_vec):
    head_count, head_width = (attended.shape[1], attended.shape[2])
    return attended * gain_vec.reshape(head_count, head_width)


def local_terms(query_feats, key_feats, values, starts, first_row):
    row_count = starts.shape[0]
    scores = jnp.einsum("thf,shf->hts", query_feats, key_feats, preferred_element_type=jnp.float32)
    position = jnp.arange(row_count)
    kept_mask = (position[None, :] <= position[:, None]) & (starts[None, :] == starts[:, None])
    scores = jnp.where(kept_mask[None], scores, jnp.zeros_like(scores))
    scores_low = scores.astype(jnp.bfloat16)
    numerator = jnp.einsum("hts,shd->thd", scores_low, values, preferred_element_type=jnp.float32)
    denominator = jnp.transpose(jnp.sum(scores, axis=2))
    in_last_doc = starts == starts[row_count - 1]
    masked_keys = jnp.where(in_last_doc[:, None, None], key_feats, jnp.zeros_like(key_feats))
    own_state = jnp.einsum("shf,shd->hfd", masked_keys, values, preferred_element_type=jnp.float32)
    own_sum = jnp.sum(masked_keys.astype(jnp.float32), axis=0)
    resets = (starts[row_count - 1] >= first_row).astype(jnp.float32)
    return (numerator, denominator, own_state, own_sum, resets)


def far_terms(query_feats, incoming, incoming_sum, from_before):
    widened = query_feats.astype(jnp.float32)
    far_numerator = jnp.einsum("thf,hfd->thd", widened, incoming, precision=lax.Precision.HIGHEST)
    far_denominator = jnp.einsum(
        "thf,hf->th", widened, incoming_sum, precision=lax.Precision.HIGHEST
    )
    return (far_numerator * from_before[:, None, None], far_denominator * from_before[:, None])


def combine_states(earlier, later):
    kept = 1.0 - later[2]
    return (
        later[0] + kept * earlier[0],
        later[1] + kept * earlier[1],
        jnp.maximum(earlier[2], later[2]),
    )


def local(tokens, norm_gain, q_weight, k_weight, v_weight, out_gain, o_weight, lengths):
    row_count = tokens.shape[0]
    head_count = q_weight.shape[1] // FEAT
    head_width = v_weight.shape[1] // head_count
    first_row = lax.axis_index("seq") * row_count
    starts = doc_starts(first_row + jnp.arange(row_count, dtype=jnp.int32), lengths)
    normed = rms_norm(tokens, norm_gain).astype(jnp.bfloat16)
    query_feats = features(
        jnp.dot(normed, q_weight, preferred_element_type=jnp.float32), head_count
    )
    key_feats = features(jnp.dot(normed, k_weight, preferred_element_type=jnp.float32), head_count)
    values = jnp.dot(normed, v_weight, preferred_element_type=jnp.float32).astype(jnp.bfloat16)
    values = values.reshape(row_count, head_count, head_width)
    numerator, denominator, own_state, own_sum, resets = local_terms(
        query_feats, key_feats, values, starts, first_row
    )
    identity = (jnp.zeros_like(own_state), jnp.zeros_like(own_sum), jnp.zeros((), jnp.float32))
    incoming, incoming_sum, _ = entering(
        (own_state, own_sum, resets), "seq", combine_states, identity
    )
    from_before = (starts < first_row).astype(jnp.float32)
    far_numerator, far_denominator = far_terms(query_feats, incoming, incoming_sum, from_before)
    attended = (numerator + far_numerator) / (denominator + far_denominator)[:, :, None]
    headed = (
        head_gain(attended, out_gain)
        .reshape(row_count, head_count * head_width)
        .astype(jnp.bfloat16)
    )
    partials = jnp.dot(headed, o_weight, preferred_element_type=jnp.float32)
    mixed = lax.psum_scatter(partials.astype(jnp.bfloat16), "mp", scatter_dimension=1, tiled=True)
    return mixed


def solution(mesh):
    placed = (
        P("seq", None),
        P(),
        P(None, "mp"),
        P(None, "mp"),
        P(None, "mp"),
        P("mp"),
        P("mp", None),
        P(),
    )
    return jax.shard_map(
        local, mesh=mesh, in_specs=placed, out_specs=P("seq", "mp"), check_vma=False
    )
```

profile of v0, /device:TPU:4, one launch (start us, length us, event | category | flops | bytes accessed | tf_op | source)
XLA Modules:
  0.0 406.1 jit_solution(13278892288122988360)
XLA Ops:
  9.5 1.9 fusion.2
  15.1 1.1 convolution_convert_fusion.2
  17.0 1.3 dynamic-slice
  19.0 125.2 %all-reduce = bf16[64]{0:T(256)(128)(2,1)S(1)} all-reduce(bf16[64]{0:T(256)(128)(2,1)S(1)} %dynamic-update-slice), channel_id=1, replica_groups=mesh['seq'=64,'mp'=8] {'seq'}, use_global_device_ids=true, to_apply=%add | all-reduce | flops 64 | bytes 256
  144.6 51.4 %all-gather.2 = bf16[64,2,273]{2,1,0:T(2,128)(2,1)S(1)} all-gather(bf16[1,2,273]{2,1,0:T(2,128)(2,1)S(1)} %bitcast.68), channel_id=3, replica_groups=mesh['seq'=64,'mp'=8] {'seq'}, dimensions={0}, use_global_device_ids=true | all-gather | bytes 70980 | tf_op jit(solution)/shard_map/all_gather | solution.py:14
  196.3 2.0 select_reduce_fusion
  198.3 151.1 %while.16 = (s32[]{:T(128)}, f32[2,273,112]{2,1,0:T(8,128)S(1)}, f32[2,273]{1,0:T(2,128)S(1)}, s32[]{:T(128)}, bf16[64,2,273,112]{3,2,1,0:T(8,128)(2,1)}, /*inde...) while((s32[]{:T(128)}, f32[2,273,112]{2,1,0:T(8,128)S(1)}, ...), condition=%wide.region_5.6_spmd.clone, body=%wide.region_4.5_spmd.clone.sunk | while | flops 308495 | bytes 617137 | solution.py:31
  201.9 1.1 fusion.36
  206.6 1.1 fusion.36
  209.0 1.1 fusion.36
  213.7 1.1 fusion.36
  216.0 1.1 fusion.36
  220.8 1.1 fusion.36
  225.5 1.1 fusion.36
  227.8 1.1 fusion.36
  232.6 1.1 fusion.36
  234.9 1.1 fusion.36
  239.6 1.1 fusion.36
  246.7 1.1 fusion.36
  251.5 1.1 fusion.36
  253.8 1.1 fusion.36
  258.5 1.1 fusion.36
  260.9 1.1 fusion.36
  265.6 1.1 fusion.36
  270.3 1.1 fusion.36
  272.7 1.1 fusion.36
  277.4 1.1 fusion.36
  279.8 1.1 fusion.36
  284.5 1.1 fusion.36
  291.6 1.1 fusion.36
  351.1 1.9 convolution_convert_fusion
  353.1 46.1 %reduce-scatter.2.cloned.1.call-done = bf16[512,224]{0,1:T(8,128)(2,1)} async-done(((bf16[512,1792]{0,1:T(8,128)(2,1)}), bf16[512,224]{0,1:T(8,128)(2,1)}) %reduce-scatter.2.cloned.1.call-update) | async-done | bytes 229392 | tf_op jit(solution)/shard_map/reduce_scatter | solution.py:128
  (215 shorter events, 92.6 us)
Async XLA Ops:
  6.5 344.6 %copy-start = (bf16[224,1792]{1,0:T(8,128)(2,1)S(1)}, bf16[224,1792]{1,0:T(8,128)(2,1)}, u32[]{:S(2)}) copy-start(bf16[224,1792]{1,0:T(8,128)(2,1)} %param.16) | copy-start | bytes 2408452
  6.5 4.9 %copy-start.1 = (bf16[512,1792]{1,0:T(8,128)(2,1)S(1)}, bf16[512,1792]{1,0:T(8,128)(2,1)}, u32[]{:S(2)}) copy-start(bf16[512,1792]{1,0:T(8,128)(2,1)} %param.10) | copy-start | bytes 5505028
  6.5 4.9 %copy-start.4 = (f32[1792]{0:T(1024)S(1)}, f32[1792]{0:T(1024)}, u32[]{:S(2)}) copy-start(f32[1792]{0:T(1024)} %param.11) | copy-start | bytes 21508
  6.5 191.7 %all-gather.5.cloned.1.call-start = ((), (), s32[]{:S(2)}) async-start(), calls=%async_computation.2 | async-start | bytes 9318400 | tf_op jit(solution)/shard_map/all_gather | solution.py:14
  11.4 0.9 copy-start.2
  12.3 0.9 copy-start.3
  13.2 1.1 copy-start.6
  15.1 1.8 copy-start.5
  16.2 383.0 %reduce-scatter.2.cloned.1.call-start = ((), (), s32[]{:S(2)}) async-start(), calls=%async_computation.1 | async-start | bytes 2064384 | tf_op jit(solution)/shard_map/reduce_scatter | solution.py:128
  349.4 1.3 copy-start.7
Sparse Core Ops, SparseCore 0:
  16.3 93.8 all-gather.4
  353.2 45.9 reduce-scatter.1
where the time goes:
time: 408 us; the launch traced here: 406 us
  blocking collectives  177 us (43%)
  other arithmetic  75.4 us (18%)
  waiting for transfers between devices  46.2 us (11%)
  loops' own time  43.6 us (11%)
  local copies, waits for them, and re-layouts  41.3 us (10%)
  between operations  14.2 us (3%)
  matrix products  8.66 us (2%)
    unnamed x1, blocking collectives  125 us
    select_n x128, other arithmetic, lap(): return jax.tree.map(lambda a, b: jnp.where(reached, a, b), new, before)  69.9 us
    all_gather x1, blocking collectives, entering(): lax.all_gather(part.astype(kind), axis)  51.4 us
    reduce_scatter x1, waiting for transfers between devices, local(): lax.psum_scatter(partials.astype(jnp.bfloat16), 'mp', scatter_dimension=1...  46.1 us
    another operation x1, loops' own time, entering(): return lax.fori_loop(0, count, lap, start)  43.6 us
    dynamic_slice x64, local copies, waits for them, and re-layouts, lap(): part[k].astype(own.dtype)  37.6 us
  transfers between devices with their start and end apart: 2, of which 1 were waited for; matrix products, arithmetic and copies ran while one was open for 1% of the time, Pallas kernels for 0%

commit v1 on v0

v1 whole, which is shorter than its diff:
```python
import functools

import jax
import jax.numpy as jnp
from jax import lax
from jax.experimental import pallas as pl
from jax.experimental.pallas import tpu as pltpu
from jax.sharding import PartitionSpec as P

MESH = pl.DeviceIdType.MESH
F32, BF16, I32 = jnp.float32, jnp.bfloat16, jnp.int32

FEAT = 16
VDIM = 112
HEADS = 2
PLANE = 8
PLANES = 8
RING = 8
TERMS = 192
CHUNK = HEADS * TERMS // PLANE
VROWS = 128

RIGHTWARD = ((4, 0), (3, 1), (3, 0), (2, 1), (2, 0), (1, 1), (1, 0))
LEFTWARD = tuple((hops, 1 - half) for hops, half in RIGHTWARD)


def dot(a, b, dims):
    return lax.dot_general(a, b, (dims, ((), ())), preferred_element_type=F32)


def write_features(out, head, u, coefficients, keep):
    square, cross, linear, constant = coefficients
    for d in range(FEAT // 2 + 1):
        turned = u if d == 0 else pltpu.roll(u, d, 0)
        scale = square if d in (0, FEAT // 2) else cross
        rows = u * turned
        if scale != 1.0:
            rows = rows * scale
        if keep is not None:
            rows = rows * keep
        out[head, d * FEAT : (d + 1) * FEAT, :] = rows.astype(BF16)
    base = (FEAT // 2 + 1) * FEAT
    rows = u * linear if linear != 1.0 else u
    if keep is not None:
        rows = rows * keep
    out[head, base : base + FEAT, :] = rows.astype(BF16)
    index = lax.broadcasted_iota(I32, (2 * FEAT, u.shape[1]), 0)
    rows = jnp.where(index == 0, constant, 0.0)
    if keep is not None:
        rows = rows * keep
    out[head, base + FEAT : base + 3 * FEAT, :] = rows.astype(BF16)


def kernel(
    tok_hbm, ng_ref, wq_hbm, wk_hbm, wv_hbm, og_ref, ow_hbm, len_ref,
    out_ref,
    tok, wq, wk, wv, ow, wcat, ot, gcol,
    vt, qt, kt, knat, qs, fk, fq, num, ht,
    st, c1, ts, c2, rs, sin, send_r, send_l, recv_r, recv_l,
    load_sem, s1, r1, s2, r2, s3, r3, ssr, rsr, ssl, rsl,
):
    rows, width = tok.shape
    half_rows = rows // 2
    seq, mp = lax.axis_index("seq"), lax.axis_index("mp")
    z, p = lax.div(seq, PLANE), lax.rem(seq, PLANE)
    first_row = seq * rows

    def in_plane(r):
        return lax.rem(p + r, PLANE)

    def along_z(r):
        return lax.rem(z + r, PLANES)

    def along_mp(r):
        return lax.rem(mp + r + RING, RING)

    barrier = pltpu.get_barrier_semaphore()
    partners = [(z * PLANE + in_plane(r), mp) for r in range(1, PLANE)]
    partners += [(along_z(r) * PLANE + p, mp) for r in range(1, PLANES)]
    partners += [(seq, along_mp(1)), (seq, along_mp(-1))]
    for who in partners:
        pl.semaphore_signal(barrier, inc=1, device_id=who, device_id_type=MESH)

    steps = 4
    step_rows = rows // steps
    loads = []
    for i, (src, dst) in enumerate(((wv_hbm, wv), (wq_hbm, wq), (wk_hbm, wk))):
        loads.append(pltpu.make_async_copy(src, dst, load_sem.at[i]))
    tok_loads = [
        pltpu.make_async_copy(
            tok_hbm.at[pl.ds(i * step_rows, step_rows), :],
            tok.at[pl.ds(i * step_rows, step_rows), :],
            load_sem.at[4 + i],
        )
        for i in range(steps)
    ]
    ow_load = pltpu.make_async_copy(ow_hbm, ow, load_sem.at[3])
    for c in loads + tok_loads + [ow_load]:
        c.start()

    lens = [len_ref[i] for i in range(len_ref.shape[0])]
    ends, total = [], None
    for n in lens:
        total = n if total is None else total + n
        ends.append(total)

    def start_of(position):
        found = 0
        for n, e in zip(lens, ends):
            found = found + jnp.where(e <= position, n, 0)
        return found

    pos_row = first_row + lax.broadcasted_iota(I32, (1, rows), 1)
    starts_row = start_of(pos_row)
    low_row = starts_row - first_row
    last_start = start_of(first_row + rows - 1)
    in_last = jnp.where(pos_row >= last_start, 1.0, 0.0).astype(F32)
    from_before = jnp.where(starts_row < first_row, 1.0, 0.0).astype(F32)

    def kept(row0, count):
        goes_on = start_of(row0 + count - 1) < row0
        return jnp.where(goes_on, 1.0, 0.0).astype(F32)

    plane_rows = PLANE * rows
    keep_p = [kept(z * plane_rows + i * rows, rows) for i in range(PLANE)]
    keep_z = [kept(i * plane_rows, plane_rows) for i in range(PLANES)]

    index = lax.broadcasted_iota(I32, (VROWS - VDIM, rows), 0)
    ones = jnp.where(index == 0, 1.0, 0.0).astype(BF16)
    for h in range(HEADS):
        vt[h, VDIM:VROWS, :] = ones
    gain_row = og_ref[...].reshape(1, HEADS * VDIM)
    gcol[...] = jnp.broadcast_to(gain_row, (128, HEADS * VDIM)).T

    for c in loads:
        c.wait()
    wcat[...] = jnp.concatenate([wv[...], wq[...]], axis=1)
    norm_gain = ng_ref[...].reshape(1, width)
    for i in range(steps):
        tok_loads[i].wait()
        cols = slice(i * step_rows, (i + 1) * step_rows)
        x = tok[cols, :].astype(F32)
        row_scale = lax.rsqrt(jnp.mean(x * x, axis=1, keepdims=True) + 1e-06)
        scaled = (x * norm_gain).astype(BF16)
        vq = dot(scaled, wcat[...], ((1,), (0,))) * row_scale
        k = dot(scaled, wk[...], ((1,), (0,))) * row_scale
        vq = vq.T
        for h in range(HEADS):
            vt[h, 0:VDIM, cols] = vq[h * VDIM : (h + 1) * VDIM, :].astype(BF16)
        qt[:, cols] = vq[HEADS * VDIM :, :]
        knat[cols, :] = k.astype(BF16)
        kt[:, cols] = k.T

    masked = in_last.astype(BF16)
    for h in range(HEADS):
        write_features(fk, h, kt[h * FEAT : (h + 1) * FEAT, :], (1.0, 1.0, 1.0, 1.0), None)
        state = dot(fk[h], vt[h] * masked, ((1,), (1,)))
        part = PLANE // HEADS
        st[h * part : (h + 1) * part] = state.astype(BF16).reshape(part, CHUNK, VROWS)

    pl.semaphore_wait(barrier, len(partners))

    sends = []

    def send(src, dst, ssem, rsem, who):
        copy = pltpu.make_async_remote_copy(
            src_ref=src, dst_ref=dst, send_sem=ssem, recv_sem=rsem,
            device_id=who, device_id_type=MESH,
        )
        copy.start()
        sends.append(copy)

    def arrived(src, dst, ssem, rsem):
        pltpu.make_async_remote_copy(
            src_ref=src, dst_ref=dst, send_sem=ssem, recv_sem=rsem,
            device_id=(seq, along_mp(1)), device_id_type=MESH,
        ).wait_recv()

    for r in range(1, PLANE):
        to = in_plane(r)
        send(st.at[to], c1.at[p], s1.at[r - 1], r1.at[r - 1], (z * PLANE + to, mp))
    c1[p] = st[p]

    for h in range(HEADS):
        u = qt[h * FEAT : (h + 1) * FEAT, :]
        write_features(fq, h, u, (1 / 16, 1 / 8, 1 / 2, 2.0), from_before)
        q4 = (u * 0.25).astype(BF16)
        zero = jnp.zeros_like(q4)
        qs[h] = jnp.concatenate([q4, zero] if h == 0 else [zero, q4], axis=0)

    for r in range(1, PLANE):
        arrived(st.at[0], c1.at[in_plane(PLANE - r)], s1.at[r - 1], r1.at[r - 1])
    run = jnp.zeros((CHUNK, VROWS), F32)
    for i in range(PLANE):
        run = run * keep_p[i] + c1[i].astype(F32)
    ts[...] = run.astype(BF16)

    for r in range(1, PLANES):
        to = along_z(r)
        send(ts, c2.at[z], s2.at[r - 1], r2.at[r - 1], (to * PLANE + p, mp))
    c2[z] = ts[...]

    def local_terms(h, half):
        t0, s_rows = half * half_rows, (half + 1) * half_rows
        t = slice(t0, t0 + half_rows)
        y = dot(knat[0:s_rows, :], qs[h, :, t], ((1,), (0,))) + 1.0
        s_index = lax.broadcasted_iota(I32, y.shape, 0)
        t_index = lax.broadcasted_iota(I32, (1, half_rows), 1) + t0
        seen = (s_index <= t_index) & (s_index >= low_row[:, t])
        weight = jnp.where(seen, y * y + 1.0, 0.0).astype(BF16)
        num[h, :, t] = dot(vt[h, :, 0:s_rows], weight, ((1,), (0,)))

    local_terms(0, 0)
    local_terms(0, 1)

    for r in range(1, PLANES):
        arrived(ts, c2.at[along_z(PLANES - r)], s2.at[r - 1], r2.at[r - 1])
    run = jnp.zeros((CHUNK, VROWS), F32)
    for i in range(PLANES):
        before = i < z
        run = run * jnp.where(before, keep_z[i], 1.0) + c2[i].astype(F32) * jnp.where(
            before, 1.0, 0.0
        )
    for i in range(PLANE):
        rs[i] = run.astype(BF16)
        if i < PLANE - 1:
            run = run * keep_p[i] + c1[i].astype(F32)

    for r in range(1, PLANE):
        to = in_plane(r)
        send(rs.at[to], sin.at[p], s3.at[r - 1], r3.at[r - 1], (z * PLANE + to, mp))
    sin[p] = rs[p]

    local_terms(1, 0)
    local_terms(1, 1)
    ow_load.wait()
    turned = ow[...].T
    ot[...] = turned.reshape(RING, HEADS * VDIM, HEADS * VDIM)

    for r in range(1, PLANE):
        arrived(rs.at[0], sin.at[in_plane(PLANE - r)], s3.at[r - 1], r3.at[r - 1])

    for half in range(2):
        t = slice(half * half_rows, (half + 1) * half_rows)
        for h in range(HEADS):
            part = PLANE // HEADS
            incoming = sin[h * part : (h + 1) * part].reshape(TERMS, VROWS)
            both = num[h, :, t] + dot(incoming, fq[h, :, t], ((0,), (0,)))
            attended = both[0:VDIM, :] * (1.0 / both[VDIM : VDIM + 1, :])
            c = slice(h * VDIM, (h + 1) * VDIM)
            gain = jnp.concatenate([gcol[c, :]] * (half_rows // 128), axis=1)
            ht[half, c, :] = (attended * gain).astype(BF16)

    def share(hops, half):
        return dot(ot[along_mp(hops)], ht[half], ((1,), (0,)))

    def ring(order, i, sign, sbuf, rbuf, ssem, rsem):
        hops, half = order[i]
        block = share(sign * hops, half)
        if (hops + 1, half) in order:
            j = order.index((hops + 1, half))
            arrived(sbuf.at[j], rbuf.at[j], ssem.at[j], rsem.at[j])
            block = block + rbuf[j].astype(F32)
        sbuf[i] = block.astype(BF16)
        send(sbuf.at[i], rbuf.at[i], ssem.at[i], rsem.at[i], (seq, along_mp(sign)))

    for i in range(len(RIGHTWARD)):
        ring(RIGHTWARD, i, 1, send_r, recv_r, ssr, rsr)
        ring(LEFTWARD, i, -1, send_l, recv_l, ssl, rsl)
    own = [share(0, half) for half in range(2)]
    for half in range(2):
        i, j = RIGHTWARD.index((1, half)), LEFTWARD.index((1, half))
        arrived(send_r.at[i], recv_r.at[i], ssr.at[i], rsr.at[i])
        arrived(send_l.at[j], recv_l.at[j], ssl.at[j], rsl.at[j])
        summed = own[half] + recv_r[i].astype(F32) + recv_l[j].astype(F32)
        out_ref[half * half_rows : (half + 1) * half_rows, :] = summed.T.astype(BF16)

    for copy in sends:
        copy.wait_send()


def local(tokens, norm_gain, q_weight, k_weight, v_weight, out_gain, o_weight, lengths):
    rows, width = tokens.shape
    wide = HEADS * VDIM
    half = (wide, rows // 2)
    dma, vmem = pltpu.SemaphoreType.DMA, pltpu.VMEM
    hbm = pl.BlockSpec(memory_space=pl.ANY)
    whole = pl.BlockSpec(memory_space=pltpu.VMEM)
    return pl.pallas_call(
        kernel,
        out_shape=jax.ShapeDtypeStruct((rows, wide), BF16),
        in_specs=[hbm, whole, hbm, hbm, hbm, whole, hbm, pl.BlockSpec(memory_space=pltpu.SMEM)],
        out_specs=whole,
        scratch_shapes=[
            vmem((rows, width), BF16),
            vmem(q_weight.shape, BF16),
            vmem(k_weight.shape, BF16),
            vmem(v_weight.shape, BF16),
            vmem(o_weight.shape, BF16),
            vmem((width, wide + HEADS * FEAT), BF16),
            vmem((RING, wide, wide), BF16),
            vmem((wide, 128), F32),
            vmem((HEADS, VROWS, rows), BF16),
            vmem((HEADS * FEAT, rows), F32),
            vmem((HEADS * FEAT, rows), F32),
            vmem((rows, HEADS * FEAT), BF16),
            vmem((HEADS, HEADS * FEAT, rows), BF16),
            vmem((HEADS, TERMS, rows), BF16),
            vmem((HEADS, TERMS, rows), BF16),
            vmem((HEADS, VROWS, rows), F32),
            vmem((2,) + half, BF16),
            vmem((PLANE, CHUNK, VROWS), BF16),
            vmem((PLANE, CHUNK, VROWS), BF16),
            vmem((CHUNK, VROWS), BF16),
            vmem((PLANES, CHUNK, VROWS), BF16),
            vmem((PLANE, CHUNK, VROWS), BF16),
            vmem((PLANE, CHUNK, VROWS), BF16),
            vmem((len(RIGHTWARD),) + half, BF16),
            vmem((len(LEFTWARD),) + half, BF16),
            vmem((len(RIGHTWARD),) + half, BF16),
            vmem((len(LEFTWARD),) + half, BF16),
            dma((8,)),
            dma((PLANE - 1,)),
            dma((PLANE - 1,)),
            dma((PLANES - 1,)),
            dma((PLANES - 1,)),
            dma((PLANE - 1,)),
            dma((PLANE - 1,)),
            dma((len(RIGHTWARD),)),
            dma((len(RIGHTWARD),)),
            dma((len(LEFTWARD),)),
            dma((len(LEFTWARD),)),
        ],
        compiler_params=pltpu.CompilerParams(
            collective_id=0, has_side_effects=True, vmem_limit_bytes=50 << 20
        ),
    )(tokens, norm_gain, q_weight, k_weight, v_weight, out_gain, o_weight, lengths)


def solution(mesh):
    placed = (
        P("seq", None),
        P(),
        P(None, "mp"),
        P(None, "mp"),
        P(None, "mp"),
        P("mp"),
        P("mp", None),
        P(),
    )
    return jax.shard_map(
        local, mesh=mesh, in_specs=placed, out_specs=P("seq", "mp"), check_vma=False
    )
```

time: 408 us -> 53.7 us (0.13)
  blocking collectives: 177 us -> 0 us
  other arithmetic: 75.4 us -> 0 us
  Pallas kernels: 0 us -> 48.7 us
  waiting for transfers between devices: 46.2 us -> 0 us
  loops' own time: 43.6 us -> 0 us
  local copies, waits for them, and re-layouts: 41.3 us -> 4.69 us
  between operations: 14.2 us -> 0.07 us
  matrix products: 8.66 us -> 0 us
    unnamed x1 -> x0, blocking collectives: 125 us -> none
    select_n x128 -> x0, other arithmetic: 69.9 us -> none  [lap(): return jax.tree.map(lambda a, b: jnp.where(reached, a, b), new, before)]
    all_gather x1 -> x0, blocking collectives: 51.4 us -> none  [entering(): lax.all_gather(part.astype(kind), axis)]
    pallas_call x0 -> x1, Pallas kernels: none -> 48.7 us  [local(): pl.pallas_call(kernel, out_shape=jax.ShapeDtypeStruct((rows, wide), BF16)...]
    reduce_scatter x1 -> x0, waiting for transfers between devices: 46.1 us -> none  [local(): lax.psum_scatter(partials.astype(jnp.bfloat16), 'mp', scatter_dimension=1...]
    another operation x1 -> x0, loops' own time: 43.6 us -> none  [entering(): return lax.fori_loop(0, count, lap, start)]
    dynamic_slice x64 -> x0, local copies, waits for them, and re-layouts: 37.6 us -> none  [lap(): part[k].astype(own.dtype)]
    dot_general x9 -> x0, matrix products: 8.66 us -> none  [the longest x1 1.99 us: local_terms(): jnp.einsum('thf,shf->hts', query_feats, key_feats, preferred_element_type...]
  transfers between devices with their start and end apart: 2 -> 0, of which waited for: 1 -> 0; matrix products, arithmetic and copies ran while one was open for 1% -> 0% of each run, Pallas kernels for 0% -> 0%
where the time goes in v1:
time: 53.7 us; the launch traced here: 53.5 us
  Pallas kernels  48.7 us (91%)
  local copies, waits for them, and re-layouts  4.69 us (9%)
    pallas_call x1, Pallas kernels, local(): pl.pallas_call(kernel, out_shape=jax.ShapeDtypeStruct((rows, wide), BF16)...  48.7 us
    unnamed x11, local copies, waits for them, and re-layouts  3.86 us

profile of v1, /device:TPU:4, one launch (start us, length us, event | category | flops | bytes accessed | tf_op | source)
XLA Modules:
  0.0 53.5 jit_solution(2433606879592096822)
XLA Ops:
  0.0 0.0 copy-start.3
  0.0 0.0 copy-start
  0.0 0.0 copy-start.2
  0.0 0.0 copy-start.1
  0.0 1.2 %copy.9.wq_hbm = bf16[1792,32]{1,0:T(8,128)(2,1)S(1)} copy(bf16[1792,32]{0,1:T(8,128)(2,1)} %param.10) | data formatting | bytes 229376 | tf_op args[2]
  1.3 1.2 %copy.10.wk_hbm = bf16[1792,32]{1,0:T(8,128)(2,1)S(1)} copy(bf16[1792,32]{0,1:T(8,128)(2,1)} %param.11) | data formatting | bytes 229376 | tf_op args[3]
  2.4 1.4 %copy.11.wv_hbm = bf16[1792,224]{1,0:T(8,128)(2,1)S(1)} copy(bf16[1792,224]{0,1:T(8,128)(2,1)} %param.12) | data formatting | bytes 1605632 | tf_op args[4]
  3.9 0.0 copy-done.3
  3.9 0.0 copy-done
  3.9 0.0 copy-done.2
  3.9 0.0 copy-done.1
  3.9 48.7 %shard_map.82 = bf16[512,224]{1,0:T(8,128)(2,1)S(1)} custom-call(bf16[512,1792]{1,0:T(8,128)(2,1)} %tok_hbm.1, f32[1792]{0:T(1024)S(1)} %copy-done.1, bf16[1792,32]{1,0:T(8,128)(2,1)S(1)} %copy.9.wq_hbm, bf16[1792,32]{1,0:T(8,128)(2,1)S(1)} %copy.10.wk_hbm, bf16[1792,224]{1,0:T(8,128)(2,1)S(1)} %copy.11.wv_hbm, f32[224]{0:T(256)S(1)} %copy-done.2, ...), custom_call_target="tpu_custom_call" | custom-call | tf_op jit(solution)/shard_map/pallas_call | solution.py:289
  52.7 0.8 %copy.12 = bf16[512,224]{0,1:T(8,128)(2,1)} copy(bf16[512,224]{1,0:T(8,128)(2,1)S(1)} %shard_map.82) | data formatting | bytes 458752 | tf_op jit(solution)/shard_map/pallas_call | solution.py:289
Async XLA Ops:
  0.0 3.9 %copy-start.3 = (s32[8]{0:T(128)S(1)}, s32[8]{0:T(128)}, u32[]{:S(2)}) copy-start(s32[8]{0:T(128)} %len_ref.1) | copy-start | bytes 100
  0.0 3.9 %copy-start = (bf16[224,1792]{1,0:T(8,128)(2,1)S(1)}, bf16[224,1792]{1,0:T(8,128)(2,1)}, u32[]{:S(2)}) copy-start(bf16[224,1792]{1,0:T(8,128)(2,1)} %ow_hbm.1) | copy-start | bytes 2408452
  0.0 3.9 %copy-start.2 = (f32[224]{0:T(256)S(1)}, f32[224]{0:T(256)}, u32[]{:S(2)}) copy-start(f32[224]{0:T(256)} %og_ref.1) | copy-start | bytes 2692
  0.0 3.9 %copy-start.1 = (f32[1792]{0:T(1024)S(1)}, f32[1792]{0:T(1024)}, u32[]{:S(2)}) copy-start(f32[1792]{0:T(1024)} %ng_ref.1) | copy-start | bytes 21508

commit v2 on v1

--- a/solution.py
+++ b/solution.py
@@ -52,9 +52,9 @@
 
 
 def kernel(
-    tok_hbm, ng_ref, wq_hbm, wk_hbm, wv_hbm, og_ref, ow_hbm, len_ref,
+    tok_hbm, ng_hbm, wq_hbm, wk_hbm, wv_hbm, og_hbm, ow_hbm, len_hbm,
     out_ref,
-    tok, wq, wk, wv, ow, wcat, ot, gcol,
+    len_ref, ng_ref, og_ref, tok, weights, ow, ot, gcol,
     vt, qt, kt, knat, qs, fk, fq, num, ht,
     st, c1, ts, c2, rs, sin, send_r, send_l, recv_r, recv_l,
     load_sem, s1, r1, s2, r2, s3, r3, ssr, rsr, ssl, rsl,
@@ -81,11 +81,16 @@
     for who in partners:
         pl.semaphore_signal(barrier, inc=1, device_id=who, device_id_type=MESH)
 
-    steps = 4
+    steps = 2
     step_rows = rows // steps
-    loads = []
-    for i, (src, dst) in enumerate(((wv_hbm, wv), (wq_hbm, wq), (wk_hbm, wk))):
+    len_load = pltpu.make_async_copy(len_hbm, len_ref, load_sem.at[6])
+    ng_load = pltpu.make_async_copy(ng_hbm, ng_ref, load_sem.at[7])
+    og_load = pltpu.make_async_copy(og_hbm, og_ref, load_sem.at[8])
+    loads, base = [], 0
+    for i, src in enumerate((wv_hbm, wq_hbm, wk_hbm)):
+        dst = weights.at[pl.ds(base, src.shape[0]), :]
         loads.append(pltpu.make_async_copy(src, dst, load_sem.at[i]))
+        base += src.shape[0]
     tok_loads = [
         pltpu.make_async_copy(
             tok_hbm.at[pl.ds(i * step_rows, step_rows), :],
@@ -95,8 +100,9 @@
         for i in range(steps)
     ]
     ow_load = pltpu.make_async_copy(ow_hbm, ow, load_sem.at[3])
-    for c in loads + tok_loads + [ow_load]:
+    for c in [len_load, ng_load] + loads + tok_loads + [og_load, ow_load]:
         c.start()
+    len_load.wait()
 
     lens = [len_ref[i] for i in range(len_ref.shape[0])]
     ends, total = [], None
@@ -129,27 +135,30 @@
     ones = jnp.where(index == 0, 1.0, 0.0).astype(BF16)
     for h in range(HEADS):
         vt[h, VDIM:VROWS, :] = ones
+    og_load.wait()
     gain_row = og_ref[...].reshape(1, HEADS * VDIM)
     gcol[...] = jnp.broadcast_to(gain_row, (128, HEADS * VDIM)).T
 
     for c in loads:
         c.wait()
-    wcat[...] = jnp.concatenate([wv[...], wq[...]], axis=1)
+    ng_load.wait()
     norm_gain = ng_ref[...].reshape(1, width)
     for i in range(steps):
         tok_loads[i].wait()
         cols = slice(i * step_rows, (i + 1) * step_rows)
         x = tok[cols, :].astype(F32)
-        row_scale = lax.rsqrt(jnp.mean(x * x, axis=1, keepdims=True) + 1e-06)
         scaled = (x * norm_gain).astype(BF16)
-        vq = dot(scaled, wcat[...], ((1,), (0,))) * row_scale
-        k = dot(scaled, wk[...], ((1,), (0,))) * row_scale
-        vq = vq.T
+        squares = x * x
+        sums = sum(squares[:, j : j + 128] for j in range(0, width, 128))
+        row_scale = lax.rsqrt(jnp.sum(sums.T, axis=0, keepdims=True) / width + 1e-06)
+        vqk = dot(weights[...], scaled, ((1,), (1,))) * row_scale
         for h in range(HEADS):
-            vt[h, 0:VDIM, cols] = vq[h * VDIM : (h + 1) * VDIM, :].astype(BF16)
-        qt[:, cols] = vq[HEADS * VDIM :, :]
-        knat[cols, :] = k.astype(BF16)
-        kt[:, cols] = k.T
+            vt[h, 0:VDIM, cols] = vqk[h * VDIM : (h + 1) * VDIM, :].astype(BF16)
+        base = HEADS * VDIM
+        qt[:, cols] = vqk[base : base + HEADS * FEAT, :]
+        k = vqk[base + HEADS * FEAT :, :]
+        kt[:, cols] = k
+        knat[cols, :] = k.T.astype(BF16)
 
     masked = in_last.astype(BF16)
     for h in range(HEADS):
@@ -273,7 +282,7 @@
         arrived(send_r.at[i], recv_r.at[i], ssr.at[i], rsr.at[i])
         arrived(send_l.at[j], recv_l.at[j], ssl.at[j], rsl.at[j])
         summed = own[half] + recv_r[i].astype(F32) + recv_l[j].astype(F32)
-        out_ref[half * half_rows : (half + 1) * half_rows, :] = summed.T.astype(BF16)
+        out_ref[:, half * half_rows : (half + 1) * half_rows] = summed.astype(BF16)
 
     for copy in sends:
         copy.wait_send()
@@ -284,20 +293,20 @@
     wide = HEADS * VDIM
     half = (wide, rows // 2)
     dma, vmem = pltpu.SemaphoreType.DMA, pltpu.VMEM
-    hbm = pl.BlockSpec(memory_space=pl.ANY)
+    hbm = pl.BlockSpec(memory_space=pltpu.HBM)
     whole = pl.BlockSpec(memory_space=pltpu.VMEM)
-    return pl.pallas_call(
+    turned = pl.pallas_call(
         kernel,
-        out_shape=jax.ShapeDtypeStruct((rows, wide), BF16),
-        in_specs=[hbm, whole, hbm, hbm, hbm, whole, hbm, pl.BlockSpec(memory_space=pltpu.SMEM)],
+        out_shape=jax.ShapeDtypeStruct((wide, rows), BF16),
+        in_specs=[hbm] * 8,
         out_specs=whole,
         scratch_shapes=[
+            pltpu.SMEM(lengths.shape, I32),
+            vmem(norm_gain.shape, F32),
+            vmem(out_gain.shape, F32),
             vmem((rows, width), BF16),
-            vmem(q_weight.shape, BF16),
-            vmem(k_weight.shape, BF16),
-            vmem(v_weight.shape, BF16),
+            vmem((wide + 2 * HEADS * FEAT, width), BF16),
             vmem(o_weight.shape, BF16),
-            vmem((width, wide + HEADS * FEAT), BF16),
             vmem((RING, wide, wide), BF16),
             vmem((wide, 128), F32),
             vmem((HEADS, VROWS, rows), BF16),
@@ -319,7 +328,7 @@
             vmem((len(LEFTWARD),) + half, BF16),
             vmem((len(RIGHTWARD),) + half, BF16),
             vmem((len(LEFTWARD),) + half, BF16),
-            dma((8,)),
+            dma((9,)),
             dma((PLANE - 1,)),
             dma((PLANE - 1,)),
             dma((PLANES - 1,)),
@@ -332,9 +341,10 @@
             dma((len(LEFTWARD),)),
         ],
         compiler_params=pltpu.CompilerParams(
-            collective_id=0, has_side_effects=True, vmem_limit_bytes=50 << 20
+            collective_id=0, has_side_effects=True, vmem_limit_bytes=58 << 20
         ),
-    )(tokens, norm_gain, q_weight, k_weight, v_weight, out_gain, o_weight, lengths)
+    )(tokens, norm_gain, q_weight.T, k_weight.T, v_weight.T, out_gain, o_weight, lengths)
+    return turned.T
 
 
 def solution(mesh):

time: 53.7 us -> 49.9 us (0.929)
  local copies, waits for them, and re-layouts: 4.69 us -> 1.64 us
  Pallas kernels: 48.7 us -> 48.1 us
    unnamed x11 -> x1, local copies, waits for them, and re-layouts: 3.86 us -> 1.64 us
    pallas_call x1 -> x0, local copies, waits for them, and re-layouts: 0.82 us -> none  [local(): pl.pallas_call(kernel, out_shape=jax.ShapeDtypeStruct((rows, wide), BF16)...]
    pallas_call x1, Pallas kernels: 48.7 us -> 48.1 us  [local(): pl.pallas_call(kernel, out_shape=jax.ShapeDtypeStruct((wide, rows), BF16)...]
where the time goes in v2:
time: 49.9 us; the launch traced here: 49.8 us
  Pallas kernels  48.1 us (96%)
  local copies, waits for them, and re-layouts  1.64 us (3%)
    pallas_call x1, Pallas kernels, local(): pl.pallas_call(kernel, out_shape=jax.ShapeDtypeStruct((wide, rows), BF16)...  48.1 us
    unnamed x1, local copies, waits for them, and re-layouts  1.64 us

profile of v2, /device:TPU:4, one launch (start us, length us, event | category | flops | bytes accessed | tf_op | source)
XLA Modules:
  0.0 49.8 jit_solution(6142833422314322726)
XLA Ops:
  0.0 48.1 %shard_map.82 = bf16[224,512]{1,0:T(8,128)(2,1)} custom-call(bf16[512,1792]{1,0:T(8,128)(2,1)} %tok_hbm.1, f32[1792]{0:T(1024)} %ng_hbm.1, bf16[32,1792]{1,0:T(8,128)(2,1)} %bitcast.6, bf16[32,1792]{1,0:T(8,128)(2,1)} %bitcast.7, bf16[224,1792]{1,0:T(8,128)(2,1)} %bitcast.5, f32[224]{0:T(256)} %og_hbm.1, bf16[224,1792]{1,0:T(8,128)(2,1)} %ow_hbm.1, s32[8]{0:T(128)} %len_hbm.1), custom_call_target="tpu_custom_call" | custom-call | tf_op jit(solution)/shard_map/pallas_call | solution.py:298
  48.1 1.6 %copy.10 = bf16[512,224]{0,1:T(8,128)(2,1)} copy(bf16[512,224]{0,1:T(8,128)(2,1)} %bitcast.4) | data formatting | bytes 458752

commit v3 on v2

--- a/solution.py
+++ b/solution.py
@@ -57,7 +57,7 @@
     len_ref, ng_ref, og_ref, tok, weights, ow, ot, gcol,
     vt, qt, kt, knat, qs, fk, fq, num, ht,
     st, c1, ts, c2, rs, sin, send_r, send_l, recv_r, recv_l,
-    load_sem, s1, r1, s2, r2, s3, r3, ssr, rsr, ssl, rsl,
+    load_sem, s1, r1, s2, r2, s3, r3, ssr, rsr, ssl, rsl, near_sem, far_sem,
 ):
     rows, width = tok.shape
     half_rows = rows // 2
@@ -74,12 +74,25 @@
     def along_mp(r):
         return lax.rem(mp + r + RING, RING)
 
+    def in_line(r):
+        return ((z + r) * PLANE + p, mp)
+
+    def on_later_planes(act, steps=range(1, PLANES)):
+        for r in steps:
+            pl.when(z + r < PLANES)(functools.partial(act, r))
+
+    def on_earlier_planes(act):
+        for r in range(1, PLANES):
+            pl.when(z >= r)(functools.partial(act, r))
+
     barrier = pltpu.get_barrier_semaphore()
     partners = [(z * PLANE + in_plane(r), mp) for r in range(1, PLANE)]
-    partners += [(along_z(r) * PLANE + p, mp) for r in range(1, PLANES)]
     partners += [(seq, along_mp(1)), (seq, along_mp(-1))]
     for who in partners:
         pl.semaphore_signal(barrier, inc=1, device_id=who, device_id_type=MESH)
+    on_later_planes(
+        lambda r: pl.semaphore_signal(barrier, inc=1, device_id=in_line(r), device_id_type=MESH)
+    )
 
     steps = 2
     step_rows = rows // steps
@@ -135,6 +148,12 @@
     ones = jnp.where(index == 0, 1.0, 0.0).astype(BF16)
     for h in range(HEADS):
         vt[h, VDIM:VROWS, :] = ones
+    for i in range(PLANES):
+
+        @pl.when(i >= z)
+        def _():
+            c2[i] = jnp.zeros((CHUNK, VROWS), BF16)
+
     og_load.wait()
     gain_row = og_ref[...].reshape(1, HEADS * VDIM)
     gcol[...] = jnp.broadcast_to(gain_row, (128, HEADS * VDIM)).T
@@ -167,23 +186,39 @@
         part = PLANE // HEADS
         st[h * part : (h + 1) * part] = state.astype(BF16).reshape(part, CHUNK, VROWS)
 
-    pl.semaphore_wait(barrier, len(partners))
+    pl.semaphore_wait(barrier, len(partners) + z)
+
+    far_half = PLANES // 2
+    upper = lax.div(z, far_half)
+
+    def say_ready(r):
+        same = lax.div(z - r, far_half) == upper
+
+        @pl.when(same)
+        def _():
+            pl.semaphore_signal(near_sem, inc=1, device_id=in_line(-r), device_id_type=MESH)
+
+        @pl.when(jnp.logical_not(same))
+        def _():
+            pl.semaphore_signal(far_sem, inc=1, device_id=in_line(-r), device_id_type=MESH)
+
+    on_earlier_planes(say_ready)
 
     sends = []
 
-    def send(src, dst, ssem, rsem, who):
-        copy = pltpu.make_async_remote_copy(
+    def remote(src, dst, ssem, rsem, who):
+        return pltpu.make_async_remote_copy(
             src_ref=src, dst_ref=dst, send_sem=ssem, recv_sem=rsem,
             device_id=who, device_id_type=MESH,
         )
+
+    def send(src, dst, ssem, rsem, who):
+        copy = remote(src, dst, ssem, rsem, who)
         copy.start()
         sends.append(copy)
 
     def arrived(src, dst, ssem, rsem):
-        pltpu.make_async_remote_copy(
-            src_ref=src, dst_ref=dst, send_sem=ssem, recv_sem=rsem,
-            device_id=(seq, along_mp(1)), device_id_type=MESH,
-        ).wait_recv()
+        remote(src, dst, ssem, rsem, (seq, along_mp(1))).wait_recv()
 
     for r in range(1, PLANE):
         to = in_plane(r)
@@ -204,10 +239,22 @@
         run = run * keep_p[i] + c1[i].astype(F32)
     ts[...] = run.astype(BF16)
 
-    for r in range(1, PLANES):
-        to = along_z(r)
-        send(ts, c2.at[z], s2.at[r - 1], r2.at[r - 1], (to * PLANE + p, mp))
-    c2[z] = ts[...]
+    def to_later(r):
+        return remote(ts, c2.at[z], s2.at[r - 1], r2.at[r - 1], in_line(r))
+
+    def to_near(r):
+        @pl.when(lax.div(z + r, far_half) == upper)
+        def _():
+            to_later(r).start()
+
+    def to_far(r):
+        @pl.when(lax.div(z + r, far_half) != upper)
+        def _():
+            to_later(r).start()
+
+    later_near = far_half - 1 - lax.rem(z, far_half)
+    pl.when(later_near > 0)(lambda: pl.semaphore_wait(near_sem, later_near))
+    on_later_planes(to_near, range(1, far_half))
 
     def local_terms(h, half):
         t0, s_rows = half * half_rows, (half + 1) * half_rows
@@ -222,14 +269,10 @@
     local_terms(0, 0)
     local_terms(0, 1)
 
-    for r in range(1, PLANES):
-        arrived(ts, c2.at[along_z(PLANES - r)], s2.at[r - 1], r2.at[r - 1])
+    on_earlier_planes(lambda r: arrived(ts, c2.at[z - r], s2.at[r - 1], r2.at[r - 1]))
     run = jnp.zeros((CHUNK, VROWS), F32)
     for i in range(PLANES):
-        before = i < z
-        run = run * jnp.where(before, keep_z[i], 1.0) + c2[i].astype(F32) * jnp.where(
-            before, 1.0, 0.0
-        )
+        run = run * jnp.where(i < z, keep_z[i], 1.0) + c2[i].astype(F32)
     for i in range(PLANE):
         rs[i] = run.astype(BF16)
         if i < PLANE - 1:
@@ -239,6 +282,8 @@
         to = in_plane(r)
         send(rs.at[to], sin.at[p], s3.at[r - 1], r3.at[r - 1], (z * PLANE + to, mp))
     sin[p] = rs[p]
+    pl.when(upper == 0)(lambda: pl.semaphore_wait(far_sem, far_half))
+    on_later_planes(to_far)
 
     local_terms(1, 0)
     local_terms(1, 1)
@@ -286,6 +331,7 @@
 
     for copy in sends:
         copy.wait_send()
+    on_later_planes(lambda r: to_later(r).wait_send())
 
 
 def local(tokens, norm_gain, q_weight, k_weight, v_weight, out_gain, o_weight, lengths):
@@ -339,6 +385,8 @@
             dma((len(RIGHTWARD),)),
             dma((len(LEFTWARD),)),
             dma((len(LEFTWARD),)),
+            pltpu.SemaphoreType.REGULAR,
+            pltpu.SemaphoreType.REGULAR,
         ],
         compiler_params=pltpu.CompilerParams(
             collective_id=0, has_side_effects=True, vmem_limit_bytes=58 << 20

time: 49.9 us -> 44.2 us (0.89)
  the two profiles are of different devices: /device:TPU:4 before, /device:TPU:384 now
where the time goes in v3:
time: 44.2 us; the launch traced here: 44.1 us
  Pallas kernels  42.4 us (96%)
  local copies, waits for them, and re-layouts  1.64 us (4%)
    pallas_call x1, Pallas kernels, local(): pl.pallas_call(kernel, out_shape=jax.ShapeDtypeStruct((wide, rows), BF16)...  42.4 us
    unnamed x1, local copies, waits for them, and re-layouts  1.64 us

profile of v3, /device:TPU:384, one launch (start us, length us, event | category | flops | bytes accessed | tf_op | source)
XLA Modules:
  0.0 44.1 jit_solution(2100758358146268069)
XLA Ops:
  0.0 42.4 %shard_map.82 = bf16[224,512]{1,0:T(8,128)(2,1)} custom-call(bf16[512,1792]{1,0:T(8,128)(2,1)} %tok_hbm.1, f32[1792]{0:T(1024)} %ng_hbm.1, bf16[32,1792]{1,0:T(8,128)(2,1)} %bitcast.6, bf16[32,1792]{1,0:T(8,128)(2,1)} %bitcast.7, bf16[224,1792]{1,0:T(8,128)(2,1)} %bitcast.5, f32[224]{0:T(256)} %og_hbm.1, bf16[224,1792]{1,0:T(8,128)(2,1)} %ow_hbm.1, s32[8]{0:T(128)} %len_hbm.1), custom_call_target="tpu_custom_call" | custom-call | tf_op jit(solution)/shard_map/pallas_call | solution.py:344
  42.4 1.6 %copy.10 = bf16[512,224]{0,1:T(8,128)(2,1)} copy(bf16[512,224]{0,1:T(8,128)(2,1)} %bitcast.4) | data formatting | bytes 458752

commit v4 on v3

--- a/solution.py
+++ b/solution.py
@@ -20,8 +20,9 @@
 CHUNK = HEADS * TERMS // PLANE
 VROWS = 128
 
-RIGHTWARD = ((4, 0), (3, 1), (3, 0), (2, 1), (2, 0), (1, 1), (1, 0))
-LEFTWARD = tuple((hops, 1 - half) for hops, half in RIGHTWARD)
+QUARTERS = 4
+RIGHTWARD = ((4, 0), (4, 1)) + tuple((k, q) for k in (3, 2, 1) for q in (2, 3, 0, 1))
+LEFTWARD = tuple((hops, (quarter + 2) % QUARTERS) for hops, quarter in RIGHTWARD)
 
 
 def dot(a, b, dims):
@@ -55,12 +56,12 @@
     tok_hbm, ng_hbm, wq_hbm, wk_hbm, wv_hbm, og_hbm, ow_hbm, len_hbm,
     out_ref,
     len_ref, ng_ref, og_ref, tok, weights, ow, ot, gcol,
-    vt, qt, kt, knat, qs, fk, fq, num, ht,
+    vt, qt, kt, knat, qs, fk, fq, num, ht, own,
     st, c1, ts, c2, rs, sin, send_r, send_l, recv_r, recv_l,
     load_sem, s1, r1, s2, r2, s3, r3, ssr, rsr, ssl, rsl, near_sem, far_sem,
 ):
     rows, width = tok.shape
-    half_rows = rows // 2
+    half_rows, quarter_rows = rows // 2, rows // QUARTERS
     seq, mp = lax.axis_index("seq"), lax.axis_index("mp")
     z, p = lax.div(seq, PLANE), lax.rem(seq, PLANE)
     first_row = seq * rows
@@ -84,15 +85,6 @@
     def on_earlier_planes(act):
         for r in range(1, PLANES):
             pl.when(z >= r)(functools.partial(act, r))
-
-    barrier = pltpu.get_barrier_semaphore()
-    partners = [(z * PLANE + in_plane(r), mp) for r in range(1, PLANE)]
-    partners += [(seq, along_mp(1)), (seq, along_mp(-1))]
-    for who in partners:
-        pl.semaphore_signal(barrier, inc=1, device_id=who, device_id_type=MESH)
-    on_later_planes(
-        lambda r: pl.semaphore_signal(barrier, inc=1, device_id=in_line(r), device_id_type=MESH)
-    )
 
     steps = 2
     step_rows = rows // steps
@@ -115,8 +107,17 @@
     ow_load = pltpu.make_async_copy(ow_hbm, ow, load_sem.at[3])
     for c in [len_load, ng_load] + loads + tok_loads + [og_load, ow_load]:
         c.start()
+
+    barrier = pltpu.get_barrier_semaphore()
+    partners = [(z * PLANE + in_plane(r), mp) for r in range(1, PLANE)]
+    partners += [(seq, along_mp(1)), (seq, along_mp(-1))]
+    for who in partners:
+        pl.semaphore_signal(barrier, inc=1, device_id=who, device_id_type=MESH)
+    on_later_planes(
+        lambda r: pl.semaphore_signal(barrier, inc=1, device_id=in_line(r), device_id_type=MESH)
+    )
+
     len_load.wait()
-
     lens = [len_ref[i] for i in range(len_ref.shape[0])]
     ends, total = [], None
     for n in lens:
@@ -157,6 +158,25 @@
     og_load.wait()
     gain_row = og_ref[...].reshape(1, HEADS * VDIM)
     gcol[...] = jnp.broadcast_to(gain_row, (128, HEADS * VDIM)).T
+
+    pl.semaphore_wait(barrier, len(partners) + z)
+
+    far_half = PLANES // 2
+    upper = lax.div(z, far_half)
+
+    def say_ready(r):
+        same = lax.div(z - r, far_half) == upper
+
+        @pl.when(same)
+        def _():
+            pl.semaphore_signal(near_sem, inc=1, device_id=in_line(-r), device_id_type=MESH)
+
+        @pl.when(jnp.logical_not(same))
+        def _():
+            pl.semaphore_signal(far_sem, inc=1, device_id=in_line(-r), device_id_type=MESH)
+
+    on_earlier_planes(say_ready)
+
 
     for c in loads:
         c.wait()
@@ -186,24 +206,6 @@
         part = PLANE // HEADS
         st[h * part : (h + 1) * part] = state.astype(BF16).reshape(part, CHUNK, VROWS)
 
-    pl.semaphore_wait(barrier, len(partners) + z)
-
-    far_half = PLANES // 2
-    upper = lax.div(z, far_half)
-
-    def say_ready(r):
-        same = lax.div(z - r, far_half) == upper
-
-        @pl.when(same)
-        def _():
-            pl.semaphore_signal(near_sem, inc=1, device_id=in_line(-r), device_id_type=MESH)
-
-        @pl.when(jnp.logical_not(same))
-        def _():
-            pl.semaphore_signal(far_sem, inc=1, device_id=in_line(-r), device_id_type=MESH)
-
-    on_earlier_planes(say_ready)
-
     sends = []
 
     def remote(src, dst, ssem, rsem, who):
@@ -302,17 +304,18 @@
             both = num[h, :, t] + dot(incoming, fq[h, :, t], ((0,), (0,)))
             attended = both[0:VDIM, :] * (1.0 / both[VDIM : VDIM + 1, :])
             c = slice(h * VDIM, (h + 1) * VDIM)
-            gain = jnp.concatenate([gcol[c, :]] * (half_rows // 128), axis=1)
-            ht[half, c, :] = (attended * gain).astype(BF16)
-
-    def share(hops, half):
-        return dot(ot[along_mp(hops)], ht[half], ((1,), (0,)))
+            for i in range(2):
+                piece = attended[:, i * quarter_rows : (i + 1) * quarter_rows] * gcol[c, :]
+                ht[2 * half + i, c, :] = piece.astype(BF16)
+
+    def share(hops, quarter):
+        return dot(ot[along_mp(hops)], ht[quarter], ((1,), (0,)))
 
     def ring(order, i, sign, sbuf, rbuf, ssem, rsem):
-        hops, half = order[i]
-        block = share(sign * hops, half)
-        if (hops + 1, half) in order:
-            j = order.index((hops + 1, half))
+        hops, quarter = order[i]
+        block = share(sign * hops, quarter)
+        if (hops + 1, quarter) in order:
+            j = order.index((hops + 1, quarter))
             arrived(sbuf.at[j], rbuf.at[j], ssem.at[j], rsem.at[j])
             block = block + rbuf[j].astype(F32)
         sbuf[i] = block.astype(BF16)
@@ -321,13 +324,15 @@
     for i in range(len(RIGHTWARD)):
         ring(RIGHTWARD, i, 1, send_r, recv_r, ssr, rsr)
         ring(LEFTWARD, i, -1, send_l, recv_l, ssl, rsl)
-    own = [share(0, half) for half in range(2)]
-    for half in range(2):
-        i, j = RIGHTWARD.index((1, half)), LEFTWARD.index((1, half))
+    for quarter in range(QUARTERS):
+        own[quarter] = share(0, quarter)
+    for quarter in (2, 0, 3, 1):
+        i, j = RIGHTWARD.index((1, quarter)), LEFTWARD.index((1, quarter))
         arrived(send_r.at[i], recv_r.at[i], ssr.at[i], rsr.at[i])
         arrived(send_l.at[j], recv_l.at[j], ssl.at[j], rsl.at[j])
-        summed = own[half] + recv_r[i].astype(F32) + recv_l[j].astype(F32)
-        out_ref[:, half * half_rows : (half + 1) * half_rows] = summed.astype(BF16)
+        summed = own[quarter] + recv_r[i].astype(F32) + recv_l[j].astype(F32)
+        cols = slice(quarter * quarter_rows, (quarter + 1) * quarter_rows)
+        out_ref[:, cols] = summed.astype(BF16)
 
     for copy in sends:
         copy.wait_send()
@@ -337,13 +342,16 @@
 def local(tokens, norm_gain, q_weight, k_weight, v_weight, out_gain, o_weight, lengths):
     rows, width = tokens.shape
     wide = HEADS * VDIM
-    half = (wide, rows // 2)
+    piece = (wide, rows // QUARTERS)
     dma, vmem = pltpu.SemaphoreType.DMA, pltpu.VMEM
     hbm = pl.BlockSpec(memory_space=pltpu.HBM)
     whole = pl.BlockSpec(memory_space=pltpu.VMEM)
+    operands = (
+        tokens, norm_gain, q_weight.T, k_weight.T, v_weight.T, out_gain, o_weight, lengths
+    )
     turned = pl.pallas_call(
         kernel,
-        out_shape=jax.ShapeDtypeStruct((wide, rows), BF16),
+        out_shape=pltpu.VMEM((wide, rows), BF16),
         in_specs=[hbm] * 8,
         out_specs=whole,
         scratch_shapes=[
@@ -363,17 +371,18 @@
             vmem((HEADS, TERMS, rows), BF16),
             vmem((HEADS, TERMS, rows), BF16),
             vmem((HEADS, VROWS, rows), F32),
-            vmem((2,) + half, BF16),
+            vmem((QUARTERS,) + piece, BF16),
+            vmem((QUARTERS,) + piece, F32),
             vmem((PLANE, CHUNK, VROWS), BF16),
             vmem((PLANE, CHUNK, VROWS), BF16),
             vmem((CHUNK, VROWS), BF16),
             vmem((PLANES, CHUNK, VROWS), BF16),
             vmem((PLANE, CHUNK, VROWS), BF16),
             vmem((PLANE, CHUNK, VROWS), BF16),
-            vmem((len(RIGHTWARD),) + half, BF16),
-            vmem((len(LEFTWARD),) + half, BF16),
-            vmem((len(RIGHTWARD),) + half, BF16),
-            vmem((len(LEFTWARD),) + half, BF16),
+            vmem((len(RIGHTWARD),) + piece, BF16),
+            vmem((len(LEFTWARD),) + piece, BF16),
+            vmem((len(RIGHTWARD),) + piece, BF16),
+            vmem((len(LEFTWARD),) + piece, BF16),
             dma((9,)),
             dma((PLANE - 1,)),
             dma((PLANE - 1,)),
@@ -389,9 +398,9 @@
             pltpu.SemaphoreType.REGULAR,
         ],
         compiler_params=pltpu.CompilerParams(
-            collective_id=0, has_side_effects=True, vmem_limit_bytes=58 << 20
+            collective_id=0, has_side_effects=True, vmem_limit_bytes=40 << 20
         ),
-    )(tokens, norm_gain, q_weight.T, k_weight.T, v_weight.T, out_gain, o_weight, lengths)
+    )(*[pltpu.with_memory_space_constraint(a, pltpu.HBM) for a in operands])
     return turned.T
 
 

time: 44.2 us -> 40.9 us (0.925)
  Pallas kernels: 42.4 us -> 40.1 us
  local copies, waits for them, and re-layouts: 1.64 us -> 0.69 us
    pallas_call x1, Pallas kernels: 42.4 us -> 40.1 us  [local(): pl.pallas_call(kernel, out_shape=pltpu.VMEM((wide, rows), BF16), in_specs...]
    unnamed x1, local copies, waits for them, and re-layouts: 1.64 us -> 0.69 us
where the time goes in v4:
time: 40.9 us; the launch traced here: 40.8 us
  Pallas kernels  40.1 us (98%)
  local copies, waits for them, and re-layouts  0.69 us (2%)
    pallas_call x1, Pallas kernels, local(): pl.pallas_call(kernel, out_shape=pltpu.VMEM((wide, rows), BF16), in_specs...  40.1 us

profile of v4, /device:TPU:384, one launch (start us, length us, event | category | flops | bytes accessed | tf_op | source)
XLA Modules:
  0.0 40.8 jit_solution(16448687656673359591)
XLA Ops:
  0.0 40.1 %shard_map.82 = bf16[224,512]{1,0:T(8,128)(2,1)S(1)} custom-call(bf16[512,1792]{1,0:T(8,128)(2,1)} %tok_hbm.1, f32[1792]{0:T(1024)} %ng_hbm.1, bf16[32,1792]{1,0:T(8,128)(2,1)} %bitcast.6, bf16[32,1792]{1,0:T(8,128)(2,1)} %bitcast.7, bf16[224,1792]{1,0:T(8,128)(2,1)} %bitcast.5, f32[224]{0:T(256)} %og_hbm.1, bf16[224,1792]{1,0:T(8,128)(2,1)} %ow_hbm.1, s32[8]{0:T(128)} %len_hbm.1), custom_call_target="tpu_custom_call" | custom-call | tf_op jit(solution)/shard_map/pallas_call | solution.py:352
  40.1 0.7 %copy.10 = bf16[512,224]{0,1:T(8,128)(2,1)} copy(bf16[512,224]{0,1:T(8,128)(2,1)S(1)} %bitcast.4) | data formatting | bytes 458752

commit v5 on v4

--- a/solution.py
+++ b/solution.py
@@ -19,6 +19,8 @@
 TERMS = 192
 CHUNK = HEADS * TERMS // PLANE
 VROWS = 128
+
+FAR_FIRST = (4, 3, 5, 2, 6, 1, 7)
 
 QUARTERS = 4
 RIGHTWARD = ((4, 0), (4, 1)) + tuple((k, q) for k in (3, 2, 1) for q in (2, 3, 0, 1))
@@ -86,7 +88,7 @@
         for r in range(1, PLANES):
             pl.when(z >= r)(functools.partial(act, r))
 
-    steps = 2
+    steps = 1
     step_rows = rows // steps
     len_load = pltpu.make_async_copy(len_hbm, len_ref, load_sem.at[6])
     ng_load = pltpu.make_async_copy(ng_hbm, ng_ref, load_sem.at[7])
@@ -105,7 +107,7 @@
         for i in range(steps)
     ]
     ow_load = pltpu.make_async_copy(ow_hbm, ow, load_sem.at[3])
-    for c in [len_load, ng_load] + loads + tok_loads + [og_load, ow_load]:
+    for c in [len_load, ng_load, tok_loads[0]] + loads + [og_load]:
         c.start()
 
     barrier = pltpu.get_barrier_semaphore()
@@ -199,6 +201,8 @@
         kt[:, cols] = k
         knat[cols, :] = k.T.astype(BF16)
 
+    ow_load.start()
+
     masked = in_last.astype(BF16)
     for h in range(HEADS):
         write_features(fk, h, kt[h * FEAT : (h + 1) * FEAT, :], (1.0, 1.0, 1.0, 1.0), None)
@@ -222,7 +226,7 @@
     def arrived(src, dst, ssem, rsem):
         remote(src, dst, ssem, rsem, (seq, along_mp(1))).wait_recv()
 
-    for r in range(1, PLANE):
+    for r in FAR_FIRST:
         to = in_plane(r)
         send(st.at[to], c1.at[p], s1.at[r - 1], r1.at[r - 1], (z * PLANE + to, mp))
     c1[p] = st[p]
@@ -280,7 +284,7 @@
         if i < PLANE - 1:
             run = run * keep_p[i] + c1[i].astype(F32)
 
-    for r in range(1, PLANE):
+    for r in FAR_FIRST:
         to = in_plane(r)
         send(rs.at[to], sin.at[p], s3.at[r - 1], r3.at[r - 1], (z * PLANE + to, mp))
     sin[p] = rs[p]

time: 40.9 us -> 39.8 us (0.973)
  Pallas kernels: 40.1 us -> 39 us
    pallas_call x1, Pallas kernels: 40.1 us -> 39 us  [local(): pl.pallas_call(kernel, out_shape=pltpu.VMEM((wide, rows), BF16), in_specs...]
where the time goes in v5:
time: 39.8 us; the launch traced here: 39.7 us
  Pallas kernels  39 us (98%)
  local copies, waits for them, and re-layouts  0.69 us (2%)
    pallas_call x1, Pallas kernels, local(): pl.pallas_call(kernel, out_shape=pltpu.VMEM((wide, rows), BF16), in_specs...  39 us

profile of v5, /device:TPU:384, one launch (start us, length us, event | category | flops | bytes accessed | tf_op | source)
XLA Modules:
  0.0 39.7 jit_solution(4183372662101889455)
XLA Ops:
  0.0 39.0 %shard_map.82 = bf16[224,512]{1,0:T(8,128)(2,1)S(1)} custom-call(bf16[512,1792]{1,0:T(8,128)(2,1)} %tok_hbm.1, f32[1792]{0:T(1024)} %ng_hbm.1, bf16[32,1792]{1,0:T(8,128)(2,1)} %bitcast.6, bf16[32,1792]{1,0:T(8,128)(2,1)} %bitcast.7, bf16[224,1792]{1,0:T(8,128)(2,1)} %bitcast.5, f32[224]{0:T(256)} %og_hbm.1, bf16[224,1792]{1,0:T(8,128)(2,1)} %ow_hbm.1, s32[8]{0:T(128)} %len_hbm.1), custom_call_target="tpu_custom_call" | custom-call | tf_op jit(solution)/shard_map/pallas_call | solution.py:356
  39.0 0.7 %copy.10 = bf16[512,224]{0,1:T(8,128)(2,1)} copy(bf16[512,224]{0,1:T(8,128)(2,1)S(1)} %bitcast.4) | data formatting | bytes 458752

commit v6 on v5

--- a/solution.py
+++ b/solution.py
@@ -23,7 +23,9 @@
 FAR_FIRST = (4, 3, 5, 2, 6, 1, 7)
 
 QUARTERS = 4
-RIGHTWARD = ((4, 0), (4, 1)) + tuple((k, q) for k in (3, 2, 1) for q in (2, 3, 0, 1))
+RIGHTWARD = ((4, 0), (3, 2), (4, 1), (3, 3), (3, 0), (3, 1)) + tuple(
+    (k, q) for k in (2, 1) for q in (2, 3, 0, 1)
+)
 LEFTWARD = tuple((hops, (quarter + 2) % QUARTERS) for hops, quarter in RIGHTWARD)
 
 

time: 39.8 us -> 39.8 us (level)
  no operation moved by 1% of the time
where the time goes in v6:
time: 39.8 us; the launch traced here: 39.7 us
  Pallas kernels  39 us (98%)
  local copies, waits for them, and re-layouts  0.69 us (2%)
    pallas_call x1, Pallas kernels, local(): pl.pallas_call(kernel, out_shape=pltpu.VMEM((wide, rows), BF16), in_specs...  39 us

profile of v6, /device:TPU:384, one launch (start us, length us, event | category | flops | bytes accessed | tf_op | source)
XLA Modules:
  0.0 39.7 jit_solution(2093262258809492366)
XLA Ops:
  0.0 39.0 %shard_map.82 = bf16[224,512]{1,0:T(8,128)(2,1)S(1)} custom-call(bf16[512,1792]{1,0:T(8,128)(2,1)} %tok_hbm.1, f32[1792]{0:T(1024)} %ng_hbm.1, bf16[32,1792]{1,0:T(8,128)(2,1)} %bitcast.6, bf16[32,1792]{1,0:T(8,128)(2,1)} %bitcast.7, bf16[224,1792]{1,0:T(8,128)(2,1)} %bitcast.5, f32[224]{0:T(256)} %og_hbm.1, bf16[224,1792]{1,0:T(8,128)(2,1)} %ow_hbm.1, s32[8]{0:T(128)} %len_hbm.1), custom_call_target="tpu_custom_call" | custom-call | tf_op jit(solution)/shard_map/pallas_call | solution.py:358
  39.0 0.7 %copy.10 = bf16[512,224]{0,1:T(8,128)(2,1)} copy(bf16[512,224]{0,1:T(8,128)(2,1)S(1)} %bitcast.4) | data formatting | bytes 458752
